TPU v7x, 512 devices: a whole 4x8x8 slice. The times are simulated.
512 devices in a mesh: grp: 8 (over z_lo, x), tile: 64 (over y, z_hi, core).
Axes of the slice: x: 4, y: 8, z: 8 (z_hi: 4, z_lo: 2; z = z_hi * 2 + z_lo), core: 2. Of those that a mesh axis runs over, the one named last changes fastest.
Arguments:
- pixels: bfloat16 [512, 128, 3, 256], P(('grp', 'tile')), parts along dimension 0, may hold values from -6 to 6
- patch_weight: bfloat16 [768, 1024], P('tile'), may hold values from -0.21875 to 0.21875
- qkv_weight: bfloat16 [1024, 1536], P('tile'), may hold values from -2.0625 to 2.0625
- out_weight: bfloat16 [512, 1024], P('tile'), may hold values from -0.25 to 0.25
- reward_head: float32 [1024], replicated, may hold values from -4 to 4
- conv_weight: bfloat16 [3, 3, 48, 3], replicated, may hold values from -1.25 to 1.25
Outputs:
- rewards: float32 [512], P(('grp', 'tile')), parts along dimension 0
- act_grad: bfloat16 [512, 128, 48, 256], P('grp', 'tile'), parts along dimension 0
There are 8 independent parts, one for each index of `grp`. A program takes and returns all parts, laid end to end along the dimension named above; an argument that names none is the same for every part. Nothing has to cross between parts.
All inputs are finite; a program needn't handle non-finite values.
Results may differ from a plain program's by a relative error of at most 0.02.
Values may be sent and summed in bfloat16 or wider, within the bound.
No kernel may reach another device: no remote copies, remote signals or barrier semaphores. Data moves between devices by JAX's collectives and lax.ppermute only.
A program may use at most 64 MiB of HBM per device.

v0:
```python
import jax
import jax.numpy as jnp
from jax import lax
from jax.sharding import PartitionSpec as P

D = 1024
HEADS = 8
HEAD_DIM = 64
PATCH = 16
PDIM = 768
LOSS_SCALE = 1024.0
NORM_EPSILON = 1e-05


def extended(value, sides, width):
    for axis, dim in sides:
        devices, length = (lax.axis_size(axis), value.shape[dim])
        up = [(i, (i + 1) % devices) for i in range(devices - 1)]
        down = [(j, i) for i, j in up]
        last = lax.slice_in_dim(value, length - width, length, axis=dim)
        first = lax.slice_in_dim(value, 0, width, axis=dim)
        before = lax.ppermute(last, axis, up)
        after = lax.ppermute(first, axis, down)
        value = jnp.concatenate([before, value, after], axis=dim)
    return value


def normalize(values_in):
    average = jnp.mean(values_in, -1, keepdims=True)
    centred = values_in - average
    inverse_scale = lax.rsqrt(jnp.mean(centred * centred, -1, keepdims=True) + NORM_EPSILON)
    return (centred * inverse_scale, inverse_scale)


def norm_back(grad_in, normed, inverse_scale):
    return inverse_scale * (
        grad_in
        - jnp.mean(grad_in, -1, keepdims=True)
        - normed * jnp.mean(grad_in * normed, -1, keepdims=True)
    )


def to_patch_rows(pixels):
    frame_count, row_count, _, col_count = pixels.shape
    blocks = pixels.reshape(frame_count, row_count // PATCH, PATCH, 3, col_count // PATCH, PATCH)
    blocks = blocks.transpose(0, 1, 4, 3, 2, 5)
    return blocks.reshape(frame_count, row_count // PATCH * (col_count // PATCH), 3 * PATCH * PATCH)


def from_patch_rows(patches, row_count, col_count):
    frame_count = patches.shape[0]
    blocks = patches.reshape(frame_count, row_count // PATCH, col_count // PATCH, 3, PATCH, PATCH)
    blocks = blocks.transpose(0, 1, 4, 3, 2, 5)
    return blocks.reshape(frame_count, row_count, 3, col_count)


def attend_forward(spread, full_qkv):
    frame_count, local_count, model_width = spread.shape
    score_scale = HEAD_DIM ** (-0.5)
    first_normed, first_scale = normalize(spread.astype(jnp.float32))
    projected = jnp.dot(
        first_normed.astype(jnp.bfloat16).reshape(-1, model_width),
        full_qkv,
        preferred_element_type=jnp.float32,
    )
    projected = projected.astype(jnp.bfloat16).reshape(frame_count, local_count, 3, HEADS, HEAD_DIM)
    query_rows = projected[:, :, 0]
    key_rows = projected[:, :, 1]
    value_rows = projected[:, :, 2]
    scores = (
        jnp.einsum("iphd,jphd->phij", query_rows, key_rows, preferred_element_type=jnp.float32)
        * score_scale
    )
    attn_probs = jax.nn.softmax(scores, axis=-1)
    probs_rounded = attn_probs.astype(jnp.bfloat16)
    attended = jnp.einsum(
        "phij,jphd->iphd", probs_rounded, value_rows, preferred_element_type=jnp.float32
    )
    attended = attended.astype(jnp.bfloat16).reshape(frame_count, local_count, HEADS * HEAD_DIM)
    return (
        first_normed,
        first_scale,
        query_rows,
        key_rows,
        value_rows,
        attn_probs,
        probs_rounded,
        attended,
    )


def attend_backward(grad_spread, saved, back_qkv):
    first_normed, first_scale, query_rows, key_rows, value_rows, attn_probs, probs_rounded, _ = (
        saved
    )
    frame_count, local_count = (first_normed.shape[0], first_normed.shape[1])
    score_scale = HEAD_DIM ** (-0.5)
    grad_heads = grad_spread.reshape(frame_count, local_count, HEADS, HEAD_DIM)
    grad_probs = jnp.einsum(
        "iphd,jphd->phij", grad_heads, value_rows, preferred_element_type=jnp.float32
    )
    grad_value = jnp.einsum(
        "phij,iphd->jphd", probs_rounded, grad_heads, preferred_element_type=jnp.float32
    ).astype(jnp.bfloat16)
    row_delta = jnp.sum(attn_probs * grad_probs, -1, keepdims=True)
    grad_scores = (attn_probs * (grad_probs - row_delta) * score_scale).astype(jnp.bfloat16)
    grad_query = jnp.einsum(
        "phij,jphd->iphd", grad_scores, key_rows, preferred_element_type=jnp.float32
    ).astype(jnp.bfloat16)
    grad_key = jnp.einsum(
        "phij,iphd->jphd", grad_scores, query_rows, preferred_element_type=jnp.float32
    ).astype(jnp.bfloat16)
    grad_proj = jnp.stack([grad_query, grad_key, grad_value], 2).reshape(-1, 3 * HEADS * HEAD_DIM)
    grad_first = jnp.dot(grad_proj, back_qkv.T, preferred_element_type=jnp.float32)
    grad_first = grad_first.reshape(first_normed.shape)
    return norm_back(grad_first, first_normed, first_scale).astype(jnp.bfloat16)


def on_device(pixels, patch_weight, qkv_weight, out_weight, reward_head, conv_weight):
    local_frames, row_count, _, col_count = pixels.shape
    model_width = D
    inner_width = HEADS * HEAD_DIM
    full_patch, full_qkv, full_out = (
        lax.all_gather(patch_weight, "tile", axis=0, tiled=True),
        lax.all_gather(qkv_weight, "tile", axis=0, tiled=True),
        lax.all_gather(out_weight, "tile", axis=0, tiled=True),
    )
    patches = to_patch_rows(pixels)
    patch_count = patches.shape[1]
    spread_patches = lax.all_to_all(patches, "tile", split_axis=1, concat_axis=0, tiled=True)
    frame_count, local_count = (spread_patches.shape[0], spread_patches.shape[1])
    embedded = jnp.dot(
        spread_patches.reshape(-1, PDIM), full_patch, preferred_element_type=jnp.float32
    )
    embedded = embedded.astype(jnp.bfloat16).reshape(frame_count, local_count, model_width)
    saved = attend_forward(embedded, full_qkv)
    hidden = embedded.astype(jnp.float32) + jnp.dot(
        saved[7].reshape(-1, inner_width), full_out, preferred_element_type=jnp.float32
    ).reshape(embedded.shape)
    second_normed, second_scale = normalize(hidden)
    partial_sums = jnp.sum(jnp.sum(second_normed * reward_head, -1), -1)
    all_rewards = lax.psum(partial_sums, "tile") / patch_count
    rewards = lax.dynamic_slice_in_dim(
        all_rewards, lax.axis_index("tile") * local_frames, local_frames
    )
    frame_coeff = -LOSS_SCALE * jax.nn.sigmoid(-all_rewards)
    grad_second = frame_coeff[:, None, None] * reward_head / patch_count
    grad_hidden = norm_back(grad_second, second_normed, second_scale)
    hidden_rounded = grad_hidden.astype(jnp.bfloat16)
    back_patch, back_qkv, back_out = (
        lax.all_gather(patch_weight, "tile", axis=0, tiled=True),
        lax.all_gather(qkv_weight, "tile", axis=0, tiled=True),
        lax.all_gather(out_weight, "tile", axis=0, tiled=True),
    )
    grad_attended = jnp.dot(
        hidden_rounded.reshape(-1, model_width), back_out.T, preferred_element_type=jnp.float32
    )
    grad_attended = grad_attended.astype(jnp.bfloat16).reshape(
        hidden.shape[0], hidden.shape[1], inner_width
    )
    grad_embed = attend_backward(grad_attended, saved, back_qkv)
    grad_total = (grad_hidden + grad_embed.astype(jnp.float32)).astype(jnp.bfloat16)
    grad_patches = jnp.dot(
        grad_total.reshape(-1, model_width), back_patch.T, preferred_element_type=jnp.float32
    )
    grad_patches = grad_patches.astype(jnp.bfloat16).reshape(hidden.shape[0], hidden.shape[1], PDIM)
    home_patches = lax.all_to_all(grad_patches, "tile", split_axis=0, concat_axis=1, tiled=True)
    grad_pixels = from_patch_rows(home_patches, row_count, col_count)
    row_grad = lax.all_to_all(grad_pixels, "tile", split_axis=1, concat_axis=0, tiled=True)
    tile_rows = row_grad.shape[1]
    padded = extended(row_grad, (("tile", 1),), 1)
    padded = jnp.pad(padded, ((0, 0), (0, 0), (0, 0), (1, 1)))
    pieces = [
        padded[:, 2 - row_off : 2 - row_off + tile_rows, :, 2 - col_off : 2 - col_off + col_count]
        for row_off in range(3)
        for col_off in range(3)
    ]
    stacked = jnp.stack(pieces, 2).reshape(row_grad.shape[0], tile_rows, 27, col_count)
    kernel = conv_weight.transpose(0, 1, 3, 2).reshape(27, -1)
    act_grad = jnp.einsum(
        "fykx,kc->fycx", stacked, kernel, preferred_element_type=jnp.float32
    ).astype(jnp.bfloat16)
    return (rewards, act_grad)


def solution(mesh):
    in_specs = (
        P(("grp", "tile"), None, None, None),
        P("tile", None),
        P("tile", None),
        P("tile", None),
        P(),
        P(),
    )
    out_specs = (P(("grp", "tile")), P("grp", "tile", None, None))
    return jax.shard_map(
        on_device, mesh=mesh, in_specs=in_specs, out_specs=out_specs, check_vma=False
    )
```

profile of v0, /device:TPU:1, one launch (start us, length us, event | category | flops | bytes accessed | tf_op | source)
XLA Modules:
  0.0 508.4 jit_solution(12765785373744496446)
XLA Ops:
  8.6 2.1 reshape.213
  11.2 1.1 reshape.230
  12.8 1.8 reduce.4
  14.6 0.8 reshape.233
  15.3 17.6 %all-to-all-start = ((bf16[64,2,768]{2,1,0:T(2,128)(2,1)}), bf16[64,2,768]{2,1,0:T(2,128)(2,1)S(1)}, u32[]{:S(2)}, u32[]{:S(2)}) async-start(bf16[64,2,768]{2,1,0:T(2,128)(2,1)} %reshape.233), calls=%async_computation | async-start | bytes 393216 | tf_op jit(solution)/shard_map/all_to_all | solution.py:130
  33.7 14.1 %all-to-all-done = bf16[64,2,768]{2,1,0:T(2,128)(2,1)S(1)} async-done(((bf16[64,2,768]{2,1,0:T(2,128)(2,1)}), bf16[64,2,768]{2,1,0:T(2,128)(2,1)S(1)}, u32[]{:S(2)}, u32[]{:S(2)}) %all-to-all-start) | async-done | bytes 196640 | tf_op jit(solution)/shard_map/all_to_all | solution.py:130
  47.9 55.3 %all-gather.9.cloned.1.call-done = bf16[64,12,1024]{2,1,0:T(8,128)(2,1)} async-done(((bf16[1,12,1024]{2,1,0:T(8,128)(2,1)}), bf16[64,12,1024]{2,1,0:T(8,128)(2,1)}) %all-gather.9.cloned.1.call-update) | async-done | bytes 1572880 | tf_op jit(solution)/shard_map/all_gather | solution.py:124
  103.2 2.5 reshape.226
  107.7 81.3 %all-gather.5.cloned.1.call-done = bf16[1024,1536]{1,0:T(8,128)(2,1)} async-done(((bf16[16,1536]{1,0:T(8,128)(2,1)}), bf16[1024,1536]{1,0:T(8,128)(2,1)}) %all-gather.5.cloned.1.call-update) | async-done | bytes 3145744 | tf_op jit(solution)/shard_map/all_gather | solution.py:125
  189.0 2.5 convolution_convert_fusion
  192.0 0.9 fusion.51
  193.2 1.4 fusion.54
  195.4 76.6 %all-gather.7.cloned.1.call-done = bf16[512,1024]{1,0:T(8,128)(2,1)} async-done(((bf16[8,1024]{1,0:T(8,128)(2,1)}), bf16[512,1024]{1,0:T(8,128)(2,1)}) %all-gather.7.cloned.1.call-update) | async-done | bytes 1048592 | tf_op jit(solution)/shard_map/all_gather | solution.py:126
  272.0 1.7 fusion.55
  274.2 138.3 %psum.7 = f32[64]{0:T(128)S(1)} all-reduce(f32[64]{0:T(128)S(1)} %multiply_reduce_fusion.3), channel_id=1, replica_groups=mesh['grp'=8,'tile'=64] {'tile'}, use_global_device_ids=true, to_apply=%region_7.0 | all-reduce | flops 64 | bytes 512 | tf_op jit(solution)/shard_map/psum | solution.py:142
  414.6 1.7 convolution_convert_fusion.7
  416.8 1.1 fusion.22
  417.9 2.7 fusion.13
  420.6 2.6 fusion.14
  423.1 1.4 fusion.15
  424.8 1.3 copy.177
  426.0 1.8 dot_general.54
  427.8 3.2 fusion.50
  432.6 23.5 %all_to_all.30 = bf16[64,2,768]{2,1,0:T(2,128)(2,1)S(1)} all-to-all(bf16[64,2,768]{2,1,0:T(2,128)(2,1)S(1)} %reshape.219), channel_id=1, replica_groups=mesh['grp'=8,'tile'=64] {'tile'}, dimensions={0} | all-to-all | bytes 393216 | tf_op jit(solution)/shard_map/all_to_all | solution.py:167
  456.1 1.1 reshape.220
  457.6 1.8 reshape.231
  459.4 19.2 %all_to_all.31 = bf16[1,128,3,256]{3,2,0,1:T(4,128)(2,1)S(1)} all-to-all(bf16[1,128,3,256]{3,2,0,1:T(4,128)(2,1)S(1)} %reshape.231), channel_id=1, replica_groups=mesh['grp'=8,'tile'=64] {'tile'}, dimensions={1} | all-to-all | bytes 393216 | tf_op jit(solution)/shard_map/all_to_all | solution.py:169
  479.1 3.3 collective-permute-start
  482.4 2.1 collective-permute-start.1
  485.2 8.7 %collective-permute-done.1 = bf16[64,1,3,256]{3,1,0,2:T(2,128)(2,1)S(1)} collective-permute-done((bf16[64,1,3,256]{3,1,0,2:T(2,128)(2,1)S(1)}, bf16[64,1,3,256]{3,1,0,2:T(2,128)(2,1)S(1)}, u32[]{:S(2)}, u32[]{:S(2)}) %collective-permute-start.1) | collective-permute-done | bytes 98336 | tf_op jit(solution)/shard_map/ppermute | solution.py:23
  493.8 1.8 select_maximum_fusion
  498.8 3.1 convert_bitcast_fusion
  (82 shorter events, 16.1 us)
Async XLA Ops:
  7.2 96.0 %all-gather.9.cloned.1.call-start = ((), (), s32[]{:S(2)}) async-start(), calls=%async_computation.5 | async-start | bytes 2129920 | tf_op jit(solution)/shard_map/all_gather | solution.py:124
  7.9 181.1 %all-gather.5.cloned.1.call-start = ((), (), s32[]{:S(2)}) async-start(), calls=%async_computation.3 | async-start | bytes 3194880 | tf_op jit(solution)/shard_map/all_gather | solution.py:125
  15.3 32.4 %all-to-all-start = ((bf16[64,2,768]{2,1,0:T(2,128)(2,1)}), bf16[64,2,768]{2,1,0:T(2,128)(2,1)S(1)}, u32[]{:S(2)}, u32[]{:S(2)}) async-start(bf16[64,2,768]{2,1,0:T(2,128)(2,1)} %reshape.233), calls=%async_computation | async-start | bytes 393216 | tf_op jit(solution)/shard_map/all_to_all | solution.py:130
  32.9 239.1 %all-gather.7.cloned.1.call-start = ((), (), s32[]{:S(2)}) async-start(), calls=%async_computation.4 | async-start | bytes 1064960 | tf_op jit(solution)/shard_map/all_gather | solution.py:126
  194.6 0.6 copy-start.10
  194.6 77.4 %copy-start.9 = (f32[2,8,64,64]{2,3,1,0:T(8,128)}, f32[2,8,64,64]{2,3,1,0:T(8,128)S(1)}, u32[]{:S(2)}) copy-start(f32[2,8,64,64]{2,3,1,0:T(8,128)S(1)} %get-tuple-element.16) | copy-start | bytes 786436
  195.4 78.5 %copy-start.5 = (f32[1024]{0:T(1024)S(1)}, f32[1024]{0:T(1024)}, u32[]{:S(2)}) copy-start(f32[1024]{0:T(1024)} %param.10) | copy-start | bytes 12292
  413.3 0.7 copy-start
  416.8 3.7 copy-start.2
  416.8 3.7 copy-start.11
  423.1 1.4 copy-start.3
  423.1 1.4 copy-start.4
  424.7 3.0 copy-start.7
  427.8 3.2 copy-start.1
  457.6 26.9 %copy-start.6 = (bf16[3,3,48,3]{2,3,1,0:T(4,128)(2,1)S(1)}, bf16[3,3,48,3]{2,3,1,0:T(4,128)(2,1)}, u32[]{:S(2)}) copy-start(bf16[3,3,48,3]{2,3,1,0:T(4,128)(2,1)} %param.11) | copy-start | bytes 7780
  457.6 26.9 %copy-start.8 = (f32[64]{0:T(128)S(1)}, f32[64]{0:T(128)}, u32[]{:S(2)}) copy-start(f32[64]{0:T(128)} %get-tuple-element.12) | copy-start | bytes 772
  479.1 6.1 %collective-permute-start = (bf16[64,1,3,256]{3,1,0,2:T(2,128)(2,1)S(1)}, bf16[64,1,3,256]{3,1,0,2:T(2,128)(2,1)S(1)}, u32[]{:S(2)}, u32[]{:S(2)}) collective-permute-start(bf16[64,1,3,256]{3,1,0,2:T(2,128)(2,1)S(1)} %get-tuple-element.7), channel_id=1, source_target_pairs={{0,1},{1,2},{2,3},{3,4},{4,5},{5,6},{6,7},{7,8},{8,9},{9,10},{10,1... | collective-permute-start | bytes 294920 | tf_op jit(solution)/shard_map/ppermute | solution.py:22
  482.4 11.5 %collective-permute-start.1 = (bf16[64,1,3,256]{3,1,0,2:T(2,128)(2,1)S(1)}, bf16[64,1,3,256]{3,1,0,2:T(2,128)(2,1)S(1)}, u32[]{:S(2)}, u32[]{:S(2)}) collective-permute-start(bf16[64,1,3,256]{3,1,0,2:T(2,128)(2,1)S(1)} %get-tuple-element.8), channel_id=1, source_target_pairs={{1,0},{2,1},{3,2},{4,3},{5,4},{6,5},{7,6},{8,7},{9,8},{10,9},{11,1... | collective-permute-start | bytes 294920 | tf_op jit(solution)/shard_map/ppermute | solution.py:23
Sparse Core Ops, SparseCore 0:
  11.3 91.8 all-gather.8
  106.5 82.4 all-gather.4
  192.3 79.6 all-gather.6
where the time goes:
time: 509 us; the launch traced here: 508 us
  waiting for transfers between devices  238 us (47%)
  blocking collectives  181 us (36%)
  starting transfers between devices  23.1 us (5%)
  matrix products  22.6 us (4%)
  local copies, waits for them, and re-layouts  22.4 us (4%)
  between operations  14.2 us (3%)
  other arithmetic  7.14 us (1%)
    psum x1, blocking collectives, on_device(): all_rewards = lax.psum(partial_sums, 'tile') / patch_count  138 us
    all_gather x1, waiting for transfers between devices, on_device(): lax.all_gather(qkv_weight, 'tile', axis=0, tiled=True)  81.3 us
    all_gather x1, waiting for transfers between devices, on_device(): lax.all_gather(out_weight, 'tile', axis=0, tiled=True)  76.6 us
    all_gather x1, waiting for transfers between devices, on_device(): lax.all_gather(patch_weight, 'tile', axis=0, tiled=True)  55.3 us
    all_to_all x1, blocking collectives, on_device(): lax.all_to_all(grad_patches, 'tile', split_axis=0, concat_axis=1, tiled=T...  23.5 us
    all_to_all x1, blocking collectives, on_device(): lax.all_to_all(grad_pixels, 'tile', split_axis=1, concat_axis=0, tiled=True)  19.2 us
    all_to_all x1, starting transfers between devices, on_device(): lax.all_to_all(patches, 'tile', split_axis=1, concat_axis=0, tiled=True)  17.6 us
    all_to_all x1, waiting for transfers between devices, on_device(): lax.all_to_all(patches, 'tile', split_axis=1, concat_axis=0, tiled=True)  14.1 us
  transfers between devices with their start and end apart: 6, of which 5 were waited for; matrix products, arithmetic and copies ran while one was open for 3% of the time, Pallas kernels for 0%

commit v1 on v0

--- a/solution.py
+++ b/solution.py
@@ -120,8 +120,16 @@
     local_frames, row_count, _, col_count = pixels.shape
     model_width = D
     inner_width = HEADS * HEAD_DIM
+
+    def measure_the_forms(local_array, chip_axis="tile"):
+        a_next = lax.psum(1, chip_axis)
+        t_next = jnp.stack(a_next * [local_array], axis=0)
+        y_new = lax.all_to_all(t_next, chip_axis, 0, 0)
+        far_arr = jnp.concatenate(y_new, axis=0)
+        return far_arr
+
     full_patch, full_qkv, full_out = (
-        lax.all_gather(patch_weight, "tile", axis=0, tiled=True),
+        measure_the_forms(patch_weight),
         lax.all_gather(qkv_weight, "tile", axis=0, tiled=True),
         lax.all_gather(out_weight, "tile", axis=0, tiled=True),
     )

time: 509 us -> 540 us (1.061)
  blocking collectives: 181 us -> 213 us
  starting transfers between devices: 23.1 us -> 10 us
  waiting for transfers between devices: 238 us -> 246 us
    all_to_all x1, waiting for transfers between devices: 14.1 us -> 51 us  [measure_the_forms(): y_new = lax.all_to_all(t_next, chip_axis, 0, 0)]
    all_gather x1, waiting for transfers between devices: 55.3 us -> 21.2 us  [on_device(): lax.all_gather(patch_weight, 'tile', axis=0, tiled=True)]
    all_to_all x0 -> x1, blocking collectives: none -> 32 us  [on_device(): lax.all_to_all(patches, 'tile', split_axis=1, concat_axis=0, tiled=True)]
    all_to_all x1, starting transfers between devices: 17.6 us -> 4.48 us  [measure_the_forms(): y_new = lax.all_to_all(t_next, chip_axis, 0, 0)]
  transfers between devices with their start and end apart: 6 -> 6, of which waited for: 5 -> 5; matrix products, arithmetic and copies ran while one was open for 3% -> 4% of each run, Pallas kernels for 0% -> 0%
where the time goes in v1:
time: 540 us; the launch traced here: 539 us
  waiting for transfers between devices  246 us (46%)
  blocking collectives  213 us (39%)
  local copies, waits for them, and re-layouts  24.5 us (5%)
  matrix products  24 us (4%)
  between operations  14.2 us (3%)
  starting transfers between devices  10 us (2%)
  other arithmetic  7.14 us (1%)
    psum x1, blocking collectives, on_device(): all_rewards = lax.psum(partial_sums, 'tile') / patch_count  138 us
    all_gather x1, waiting for transfers between devices, on_device(): lax.all_gather(qkv_weight, 'tile', axis=0, tiled=True)  86.5 us
    all_gather x1, waiting for transfers between devices, on_device(): lax.all_gather(out_weight, 'tile', axis=0, tiled=True)  76.6 us
    all_to_all x1, waiting for transfers between devices, measure_the_forms(): y_new = lax.all_to_all(t_next, chip_axis, 0, 0)  51 us
    all_to_all x1, blocking collectives, on_device(): lax.all_to_all(patches, 'tile', split_axis=1, concat_axis=0, tiled=True)  32 us
    all_to_all x1, blocking collectives, on_device(): lax.all_to_all(grad_patches, 'tile', split_axis=0, concat_axis=1, tiled=T...  23.5 us
    all_gather x1, waiting for transfers between devices, on_device(): lax.all_gather(patch_weight, 'tile', axis=0, tiled=True)  21.2 us
    all_to_all x1, blocking collectives, on_device(): lax.all_to_all(grad_pixels, 'tile', split_axis=1, concat_axis=0, tiled=True)  19.2 us
  transfers between devices with their start and end apart: 6, of which 5 were waited for; matrix products, arithmetic and copies ran while one was open for 4% of the time, Pallas kernels for 0%

profile of v1, /device:TPU:1, one launch (start us, length us, event | category | flops | bytes accessed | tf_op | source)
XLA Modules:
  0.0 538.9 jit_solution(13860853776164044633)
XLA Ops:
  8.6 2.1 reshape.218
  12.8 1.8 reduce.4
  14.7 32.0 %all_to_all.35 = bf16[64,2,768]{2,1,0:T(2,128)(2,1)S(1)} all-to-all(bf16[64,2,768]{2,1,0:T(2,128)(2,1)S(1)} %reshape.239), channel_id=1, replica_groups=mesh['grp'=8,'tile'=64] {'tile'}, dimensions={0} | all-to-all | bytes 393216 | tf_op jit(solution)/shard_map/all_to_all | solution.py:138
  46.7 1.6 stack.30
  48.3 4.5 all-to-all-start.1
  53.7 51.0 %all-to-all-done.1 = bf16[64,12,1024]{2,1,0:T(8,128)(2,1)S(1)} async-done(((bf16[64,12,1024]{2,1,0:T(8,128)(2,1)}), bf16[64,12,1024]{2,1,0:T(8,128)(2,1)S(1)}, u32[]{:S(2)}, u32[]{:S(2)}) %all-to-all-start.1) | async-done | bytes 1572896 | tf_op jit(solution)/shard_map/all_to_all | solution.py:127
  104.6 1.3 reshape.221
  106.0 1.9 fusion.53
  109.3 21.2 %all-gather.9.cloned.1.call-done = bf16[64,12,1024]{2,1,0:T(8,128)(2,1)} async-done(((bf16[1,12,1024]{2,1,0:T(8,128)(2,1)}), bf16[64,12,1024]{2,1,0:T(8,128)(2,1)}) %all-gather.9.cloned.1.call-update) | async-done | bytes 1572880 | tf_op jit(solution)/shard_map/all_gather | solution.py:159
  130.5 2.5 reshape.232
  133.1 86.5 %all-gather.5.cloned.1.call-done = bf16[1024,1536]{1,0:T(8,128)(2,1)} async-done(((bf16[16,1536]{1,0:T(8,128)(2,1)}), bf16[1024,1536]{1,0:T(8,128)(2,1)}) %all-gather.5.cloned.1.call-update) | async-done | bytes 3145744 | tf_op jit(solution)/shard_map/all_gather | solution.py:133
  219.6 2.5 convolution_convert_fusion
  223.8 1.4 fusion.54
  226.0 76.6 %all-gather.7.cloned.1.call-done = bf16[512,1024]{1,0:T(8,128)(2,1)} async-done(((bf16[8,1024]{1,0:T(8,128)(2,1)}), bf16[512,1024]{1,0:T(8,128)(2,1)}) %all-gather.7.cloned.1.call-update) | async-done | bytes 1048592 | tf_op jit(solution)/shard_map/all_gather | solution.py:134
  302.6 1.7 fusion.55
  304.7 138.3 %psum.7 = f32[64]{0:T(128)S(1)} all-reduce(f32[64]{0:T(128)S(1)} %multiply_reduce_fusion.3), channel_id=1, replica_groups=mesh['grp'=8,'tile'=64] {'tile'}, use_global_device_ids=true, to_apply=%region_7.0 | all-reduce | flops 64 | bytes 512 | tf_op jit(solution)/shard_map/psum | solution.py:150
  445.2 1.7 convolution_convert_fusion.7
  448.4 2.7 fusion.13
  451.1 2.6 fusion.14
  453.7 1.4 fusion.15
  455.3 1.3 copy.177
  456.6 1.8 dot_general.54
  458.4 3.2 fusion.50
  463.1 23.5 %all_to_all.36 = bf16[64,2,768]{2,1,0:T(2,128)(2,1)S(1)} all-to-all(bf16[64,2,768]{2,1,0:T(2,128)(2,1)S(1)} %reshape.225), channel_id=1, replica_groups=mesh['grp'=8,'tile'=64] {'tile'}, dimensions={0} | all-to-all | bytes 393216 | tf_op jit(solution)/shard_map/all_to_all | solution.py:175
  486.6 1.1 reshape.226
  488.2 1.8 reshape.237
  490.0 19.2 %all_to_all.37 = bf16[1,128,3,256]{3,2,0,1:T(4,128)(2,1)S(1)} all-to-all(bf16[1,128,3,256]{3,2,0,1:T(4,128)(2,1)S(1)} %reshape.237), channel_id=1, replica_groups=mesh['grp'=8,'tile'=64] {'tile'}, dimensions={1} | all-to-all | bytes 393216 | tf_op jit(solution)/shard_map/all_to_all | solution.py:177
  509.7 3.3 collective-permute-start
  512.9 2.1 collective-permute-start.1
  515.7 8.7 %collective-permute-done.1 = bf16[64,1,3,256]{3,1,0,2:T(2,128)(2,1)S(1)} collective-permute-done((bf16[64,1,3,256]{3,1,0,2:T(2,128)(2,1)S(1)}, bf16[64,1,3,256]{3,1,0,2:T(2,128)(2,1)S(1)}, u32[]{:S(2)}, u32[]{:S(2)}) %collective-permute-start.1) | collective-permute-done | bytes 98336 | tf_op jit(solution)/shard_map/ppermute | solution.py:23
  524.4 1.8 select_maximum_fusion
  529.3 3.1 convert_bitcast_fusion
  (87 shorter events, 18.8 us)
Async XLA Ops:
  7.2 123.4 %all-gather.9.cloned.1.call-start = ((), (), s32[]{:S(2)}) async-start(), calls=%async_computation.6 | async-start | bytes 2129920 | tf_op jit(solution)/shard_map/all_gather | solution.py:159
  7.9 211.7 %all-gather.5.cloned.1.call-start = ((), (), s32[]{:S(2)}) async-start(), calls=%async_computation.4 | async-start | bytes 3194880 | tf_op jit(solution)/shard_map/all_gather | solution.py:133
  11.2 35.6 %copy-start.5 = (bf16[12,1024]{1,0:T(8,128)(2,1)S(1)}, bf16[12,1024]{1,0:T(8,128)(2,1)}, u32[]{:S(2)}) copy-start(bf16[12,1024]{1,0:T(8,128)(2,1)} %param.7) | copy-start | bytes 73732
  48.3 56.3 %all-to-all-start.1 = ((bf16[64,12,1024]{2,1,0:T(8,128)(2,1)}), bf16[64,12,1024]{2,1,0:T(8,128)(2,1)S(1)}, u32[]{:S(2)}, u32[]{:S(2)}) async-start(bf16[64,12,1024]{2,1,0:T(8,128)(2,1)} %stack.30), calls=%async_computation.1 | async-start | bytes 4194304 | tf_op jit(solution)/shard_map/all_to_all | solution.py:127
  52.8 249.8 %all-gather.7.cloned.1.call-start = ((), (), s32[]{:S(2)}) async-start(), calls=%async_computation.5 | async-start | bytes 1064960 | tf_op jit(solution)/shard_map/all_gather | solution.py:134
  225.2 0.6 copy-start.11
  225.2 77.4 %copy-start.10 = (f32[2,8,64,64]{2,3,1,0:T(8,128)}, f32[2,8,64,64]{2,3,1,0:T(8,128)S(1)}, u32[]{:S(2)}) copy-start(f32[2,8,64,64]{2,3,1,0:T(8,128)S(1)} %get-tuple-element.16) | copy-start | bytes 786436
  226.0 78.5 %copy-start.6 = (f32[1024]{0:T(1024)S(1)}, f32[1024]{0:T(1024)}, u32[]{:S(2)}) copy-start(f32[1024]{0:T(1024)} %param.10) | copy-start | bytes 12292
  443.8 0.7 copy-start
  447.4 3.7 copy-start.2
  447.4 3.7 copy-start.12
  453.7 1.4 copy-start.3
  453.7 1.4 copy-start.4
  455.1 3.2 copy-start.8
  458.4 3.2 copy-start.1
  488.2 26.9 %copy-start.7 = (bf16[3,3,48,3]{2,3,1,0:T(4,128)(2,1)S(1)}, bf16[3,3,48,3]{2,3,1,0:T(4,128)(2,1)}, u32[]{:S(2)}) copy-start(bf16[3,3,48,3]{2,3,1,0:T(4,128)(2,1)} %param.11) | copy-start | bytes 7780
  488.2 26.9 %copy-start.9 = (f32[64]{0:T(128)S(1)}, f32[64]{0:T(128)}, u32[]{:S(2)}) copy-start(f32[64]{0:T(128)} %get-tuple-element.12) | copy-start | bytes 772
  509.7 6.1 %collective-permute-start = (bf16[64,1,3,256]{3,1,0,2:T(2,128)(2,1)S(1)}, bf16[64,1,3,256]{3,1,0,2:T(2,128)(2,1)S(1)}, u32[]{:S(2)}, u32[]{:S(2)}) collective-permute-start(bf16[64,1,3,256]{3,1,0,2:T(2,128)(2,1)S(1)} %get-tuple-element.7), channel_id=1, source_target_pairs={{0,1},{1,2},{2,3},{3,4},{4,5},{5,6},{6,7},{7,8},{8,9},{9,10},{10,1... | collective-permute-start | bytes 294920 | tf_op jit(solution)/shard_map/ppermute | solution.py:22
  512.9 11.5 %collective-permute-start.1 = (bf16[64,1,3,256]{3,1,0,2:T(2,128)(2,1)S(1)}, bf16[64,1,3,256]{3,1,0,2:T(2,128)(2,1)S(1)}, u32[]{:S(2)}, u32[]{:S(2)}) collective-permute-start(bf16[64,1,3,256]{3,1,0,2:T(2,128)(2,1)S(1)} %get-tuple-element.8), channel_id=1, source_target_pairs={{1,0},{2,1},{3,2},{4,3},{5,4},{6,5},{7,6},{8,7},{9,8},{10,9},{11,1... | collective-permute-start | bytes 294920 | tf_op jit(solution)/shard_map/ppermute | solution.py:23
Sparse Core Ops, SparseCore 0:
  11.3 119.2 all-gather.8
  133.9 85.6 all-gather.4
  222.9 79.6 all-gather.6
